TPU v7x, 256 devices: a whole 4x4x8 slice. The times are simulated.
256 devices in a mesh: expert: 8 (over z), tp: 8 (over x, core), dp: 4 (over y).
Axes of the slice: x: 4, y: 4, z: 8, core: 2. Of those that a mesh axis runs over, the one named last changes fastest.
Arguments:
- hidden: bfloat16 [1024, 6144], P(('expert', 'tp', 'dp')), may hold values from -400 to 400
- norm_gain: float32 [6144], replicated, may hold values from 0.1 to 1.9
- expert_ids: int32 [1024, 2], P(('expert', 'tp', 'dp')), may hold values from 0 to 7, all different within a row; in each aligned block of 4 rows (0 to 3, 4 to 7, ...) at most 2 rows name the same one
- router_logits: float32 [1024, 2], P(('expert', 'tp', 'dp')), may hold values from -6 to 6
- w_gate: bfloat16 [8, 6144, 8192], P('expert', None, ('tp', 'dp')), may hold values from -0.078125 to 0.078125
- w_up: bfloat16 [8, 6144, 8192], P('expert', None, ('tp', 'dp')), may hold values from -0.078125 to 0.078125
- w_down: bfloat16 [8, 8192, 6144], P('expert', ('tp', 'dp')), may hold values from -0.0625 to 0.0625
Outputs:
- moe_out: bfloat16 [1024, 6144], P(('expert', 'tp', 'dp'))
Inputs may be any that keep to these rules, and one draw needn't show every extreme that they name: `expert_ids`: each token names two different experts; the tokens of one device name one expert at most 2 times.
All inputs are finite; a program needn't handle non-finite values.
Results may differ from a plain program's by a relative error of at most 0.015.
Values may be sent and summed in bfloat16 or wider, within the bound.
No kernel may reach another device: no remote copies, remote signals or barrier semaphores. Data moves between devices by JAX's collectives and lax.ppermute only.
A program may use at most 64 MiB of HBM per device.

v0:
```python
import jax
import jax.numpy as jnp
from jax import lax
from jax.sharding import PartitionSpec as P

MOST = 2


def joined_along(pieces, dim):
    pieces = jnp.moveaxis(pieces, 0, dim)
    dims = pieces.shape
    return pieces.reshape(*dims[:dim], dims[dim] * dims[dim + 1], *dims[dim + 2 :])


def copy_for_each(shard, axis):
    peers = lax.axis_size(axis)
    return lax.all_to_all(
        jnp.broadcast_to(shard[None], (peers, *shard.shape)), axis, 0, 0, tiled=True
    )


def collect(shard, axis, dim):
    return joined_along(copy_for_each(shard, axis), dim)


def in_blocks(shard, dim, peers):
    before, after = (shard.shape[:dim], shard.shape[dim + 1 :])
    return jnp.moveaxis(shard.reshape(*before, peers, -1, *after), dim, 0)


def summed_on_arrival(shard, axis, dim):
    pieces = in_blocks(shard, dim, lax.axis_size(axis))
    arrived = lax.all_to_all(pieces, axis, split_axis=0, concat_axis=0, tiled=True)
    return arrived.astype(jnp.float32).sum(axis=0)


def body(hidden, norm_gain, expert_ids, router_logits, w_gate, w_up, w_down):
    width = hidden.shape[1]
    values = hidden.astype(jnp.float32)
    inverse = lax.rsqrt(jnp.mean(values * values, axis=1, keepdims=True) + 1e-05)
    normed = (values * inverse * norm_gain[None, :]).astype(jnp.bfloat16)
    groups = lax.axis_size("expert")
    assigned = expert_ids.reshape(-1)
    onehot = (assigned[:, None] == jnp.arange(groups, dtype=jnp.int32)[None, :]).astype(jnp.int32)
    earlier = jnp.cumsum(onehot, axis=0) - onehot
    position = jnp.sum(earlier * onehot, axis=1)
    chosen = assigned[None, None, :] == jnp.arange(groups, dtype=jnp.int32)[:, None, None]
    placed = position[None, None, :] == jnp.arange(MOST, dtype=jnp.int32)[None, :, None]
    selector = (chosen & placed).astype(jnp.bfloat16).reshape(groups * MOST, assigned.shape[0])
    repeated = jnp.repeat(normed, 2, axis=0)
    bucket = jnp.dot(selector, repeated, preferred_element_type=jnp.float32).astype(jnp.bfloat16)
    arrived = lax.all_to_all(
        bucket.reshape(groups, MOST, width), "expert", split_axis=0, concat_axis=0, tiled=True
    )
    arrived = arrived.reshape(groups * MOST, width)
    gate_mat = w_gate[0]
    up_mat = w_up[0]
    down_mat = w_down[0]
    nearby = collect(arrived, "dp", 0)
    block_rows = lax.all_gather(nearby, "tp", axis=0, tiled=True)
    gate_val = jnp.dot(block_rows, gate_mat, preferred_element_type=jnp.float32)
    up_val = jnp.dot(block_rows, up_mat, preferred_element_type=jnp.float32)
    activations = (jax.nn.silu(gate_val) * up_val).astype(jnp.bfloat16)
    partial_sum = lax.psum_scatter(
        jnp.dot(activations, down_mat, preferred_element_type=jnp.float32).astype(jnp.bfloat16),
        "tp",
        scatter_dimension=0,
        tiled=True,
    )
    summed = summed_on_arrival(partial_sum, "dp", 0)
    outgoing = summed.astype(jnp.bfloat16).reshape(groups, MOST, width)
    returned = lax.all_to_all(outgoing, "expert", split_axis=0, concat_axis=0, tiled=True)
    picked = jnp.dot(
        selector.T, returned.reshape(groups * MOST, width), preferred_element_type=jnp.float32
    )
    picked = picked.reshape(hidden.shape[0], 2, width)
    first = jax.nn.sigmoid(router_logits[:, 0] - router_logits[:, 1])
    second = jax.nn.sigmoid(router_logits[:, 1] - router_logits[:, 0])
    route_weight = jnp.stack([first, second], axis=1)
    combined = jnp.sum(picked * route_weight[:, :, None], axis=1)
    return combined.astype(jnp.bfloat16)


def solution(mesh):
    placed = (
        P(("expert", "tp", "dp"), None),
        P(),
        P(("expert", "tp", "dp"), None),
        P(("expert", "tp", "dp"), None),
        P("expert", None, ("tp", "dp")),
        P("expert", None, ("tp", "dp")),
        P("expert", ("tp", "dp"), None),
    )
    return jax.shard_map(
        body, mesh=mesh, in_specs=placed, out_specs=P(("expert", "tp", "dp"), None), check_vma=False
    )
```

profile of v0, /device:TPU:6, one launch (start us, length us, event | category | flops | bytes accessed | tf_op | source)
XLA Modules:
  0.0 184.7 jit_solution(16273812825618308525)
XLA Ops:
  6.5 0.9 copy.14
  7.5 0.1 eq.51
  7.6 0.2 select_reduce_fusion
  7.9 1.0 fusion.12
  8.8 0.9 fusion.14
  9.9 0.2 convolution_convert_fusion.1
  10.0 0.1 reshape.96
  10.2 18.7 %all_to_all.20 = bf16[8,2,6144]{2,1,0:T(2,128)(2,1)S(1)} all-to-all(bf16[8,2,6144]{2,1,0:T(2,128)(2,1)S(1)} %reshape.96), channel_id=1, replica_groups=mesh['expert'=8,'tp'=8,'dp'=4] {'expert'}, dimensions={0} | all-to-all | bytes 393216 | tf_op jit(solution)/shard_map/all_to_all | solution.py:52
  28.9 0.1 broadcast_in_dim.7
  29.1 14.9 %all_to_all.21 = bf16[4,16,6144]{2,1,0:T(8,128)(2,1)} all-to-all(bf16[4,16,6144]{2,1,0:T(8,128)(2,1)S(1)} %broadcast_in_dim.8), channel_id=1, replica_groups=mesh['expert'=8,'tp'=8,'dp'=4] {'dp'}, dimensions={0} | all-to-all | bytes 1572864 | tf_op jit(solution)/shard_map/all_to_all | solution.py:17
  44.1 37.3 %all-gather.2.cloned.1.call-done = bf16[512,6144]{1,0:T(8,128)(2,1)} async-done(((bf16[64,6144]{1,0:T(8,128)(2,1)}), bf16[512,6144]{1,0:T(8,128)(2,1)}) %all-gather.2.cloned.1.call-update) | async-done | bytes 6291472 | tf_op jit(solution)/shard_map/all_gather | solution.py:60
  81.3 5.6 %fusion.3 = f32[512,256]{1,0:T(8,128)S(1)} fusion(bf16[512,6144]{1,0:T(8,128)(2,1)} %all-gather.2.cloned.1.call-done, bf16[1,6144,256]{2,1,0:T(8,128)(2,1)} %param.11), kind=kOutput, calls=%fused_computation.6 | convolution fusion | flops 1610612736 | bytes 9961472 | tf_op jit(solution)/shard_map/dot_general | solution.py:61
  87.0 0.8 copy-done.3
  87.8 1.8 fusion.8
  89.6 4.5 %convolution_convert_fusion = bf16[512,6144]{1,0:T(8,128)(2,1)} fusion(bf16[512,256]{1,0:T(8,128)(2,1)S(1)} %fusion.8, bf16[1,256,6144]{2,1,0:T(8,128)(2,1)S(1)} %copy-done), kind=kOutput, calls=%fused_computation | convolution fusion | flops 1613758464 | bytes 9699328 | tf_op jit(solution)/shard_map/dot_general | solution.py:65
  94.1 45.3 %reduce-scatter.2.cloned.1.call-done = bf16[64,6144]{1,0:T(8,128)(2,1)} async-done(((bf16[512,6144]{1,0:T(8,128)(2,1)}), bf16[64,6144]{1,0:T(8,128)(2,1)}) %reduce-scatter.2.cloned.1.call-update) | async-done | bytes 786448 | tf_op jit(solution)/shard_map/reduce_scatter | solution.py:64
  139.3 17.9 %all_to_all.22 = bf16[4,16,6144]{2,1,0:T(8,128)(2,1)} all-to-all(bf16[4,16,6144]{2,1,0:T(8,128)(2,1)} %bitcast.23), channel_id=1, replica_groups=mesh['expert'=8,'tp'=8,'dp'=4] {'dp'}, dimensions={0} | all-to-all | bytes 1572864 | tf_op jit(solution)/shard_map/all_to_all | solution.py:33
  157.3 1.3 reduce_sum.41
  158.6 0.8 reshape.99
  159.4 7.0 %all-to-all-start.3 = ((bf16[8,2,6144]{2,1,0:T(2,128)(2,1)}), bf16[8,2,6144]{2,1,0:T(2,128)(2,1)S(1)}, u32[]{:S(2)}, u32[]{:S(2)}) async-start(bf16[8,2,6144]{2,1,0:T(2,128)(2,1)} %reshape.99), calls=%async_computation.4 | async-start | bytes 393216 | tf_op jit(solution)/shard_map/all_to_all | solution.py:72
  166.4 0.1 copy.15
  166.5 10.5 %all-to-all-done.3 = bf16[8,2,6144]{2,1,0:T(2,128)(2,1)S(1)} async-done(((bf16[8,2,6144]{2,1,0:T(2,128)(2,1)}), bf16[8,2,6144]{2,1,0:T(2,128)(2,1)S(1)}, u32[]{:S(2)}, u32[]{:S(2)}) %all-to-all-start.3) | async-done | bytes 196640 | tf_op jit(solution)/shard_map/all_to_all | solution.py:72
  177.0 0.1 reshape.101
  177.1 0.8 fusion.11
  (23 shorter events, 0.4 us)
Async XLA Ops:
  6.5 83.0 %copy-start = (bf16[1,256,6144]{2,1,0:T(8,128)(2,1)S(1)}, bf16[1,256,6144]{2,1,0:T(8,128)(2,1)}, u32[]{:S(2)}) copy-start(bf16[1,256,6144]{2,1,0:T(8,128)(2,1)} %param.13) | copy-start | bytes 9437188
  6.5 74.8 %all-gather.2.cloned.1.call-start = ((), (), s32[]{:S(2)}) async-start(), calls=%async_computation.5 | async-start | bytes 7077888 | tf_op jit(solution)/shard_map/all_gather | solution.py:60
  44.0 95.3 %reduce-scatter.2.cloned.1.call-start = ((), (), s32[]{:S(2)}) async-start(), calls=%async_computation.6 | async-start | bytes 7077888 | tf_op jit(solution)/shard_map/reduce_scatter | solution.py:64
  81.3 5.7 %copy-start.2 = (bf16[512,6144]{1,0:T(8,128)(2,1)S(1)}, bf16[512,6144]{1,0:T(8,128)(2,1)}, u32[]{:S(2)}) copy-start(bf16[512,6144]{1,0:T(8,128)(2,1)} %all-gather.2.cloned.1.call-done) | copy-start | bytes 18874372
  81.3 6.4 %copy-start.3 = (bf16[1,6144,256]{2,1,0:T(8,128)(2,1)S(1)}, bf16[1,6144,256]{2,1,0:T(8,128)(2,1)}, u32[]{:S(2)}) copy-start(bf16[1,6144,256]{2,1,0:T(8,128)(2,1)} %param.12) | copy-start | bytes 9437188
  94.1 72.4 %copy-start.1 = (f32[4,2]{0,1:T(2,128)S(1)}, f32[4,2]{0,1:T(2,128)}, u32[]{:S(2)}) copy-start(f32[4,2]{0,1:T(2,128)} %param.10) | copy-start | bytes 100
  159.4 17.6 %all-to-all-start.3 = ((bf16[8,2,6144]{2,1,0:T(2,128)(2,1)}), bf16[8,2,6144]{2,1,0:T(2,128)(2,1)S(1)}, u32[]{:S(2)}, u32[]{:S(2)}) async-start(bf16[8,2,6144]{2,1,0:T(2,128)(2,1)} %reshape.99), calls=%async_computation.4 | async-start | bytes 393216 | tf_op jit(solution)/shard_map/all_to_all | solution.py:72
Sparse Core Ops, SparseCore 0:
  44.1 37.1 all-gather.1
  94.2 45.1 reduce-scatter.1
where the time goes:
time: 185 us
  waiting for transfers between devices  93.1 us (50%)
  blocking collectives  51.6 us (28%)
  between operations  13.5 us (7%)
  matrix products  12.9 us (7%)
  starting transfers between devices  7.05 us (4%)
  other arithmetic  3.5 us (2%)
  local copies, waits for them, and re-layouts  3.15 us (2%)
    reduce_scatter x1, waiting for transfers between devices, body(): lax.psum_scatter(jnp.dot(activations, down_mat, preferred_element_type=jn...  45.3 us
    all_gather x1, waiting for transfers between devices, body(): block_rows = lax.all_gather(nearby, 'tp', axis=0, tiled=True)  37.3 us
    all_to_all x1, blocking collectives, body(): lax.all_to_all(bucket.reshape(groups, MOST, width), 'expert', split_axis=...  18.7 us
    all_to_all x1, blocking collectives, summed_on_arrival(): lax.all_to_all(pieces, axis, split_axis=0, concat_axis=0, tiled=True)  17.9 us
    all_to_all x1, blocking collectives, copy_for_each(): lax.all_to_all(jnp.broadcast_to(shard[None], (peers, *shard.shape)), axis...  14.9 us
    all_to_all x1, waiting for transfers between devices, body(): lax.all_to_all(outgoing, 'expert', split_axis=0, concat_axis=0, tiled=True)  10.5 us
    all_to_all x1, starting transfers between devices, body(): lax.all_to_all(outgoing, 'expert', split_axis=0, concat_axis=0, tiled=True)  7.01 us
    dot_general x1, matrix products, body(): gate_val = jnp.dot(block_rows, gate_mat, preferred_element_type=jnp.float32)  5.64 us
  transfers between devices with their start and end apart: 3, of which 3 were waited for; matrix products, arithmetic and copies ran while one was open for 0% of the time, Pallas kernels for 0%

commit v1 on v0

--- a/solution.py
+++ b/solution.py
@@ -4,34 +4,6 @@
 from jax.sharding import PartitionSpec as P
 
 MOST = 2
-
-
-def joined_along(pieces, dim):
-    pieces = jnp.moveaxis(pieces, 0, dim)
-    dims = pieces.shape
-    return pieces.reshape(*dims[:dim], dims[dim] * dims[dim + 1], *dims[dim + 2 :])
-
-
-def copy_for_each(shard, axis):
-    peers = lax.axis_size(axis)
-    return lax.all_to_all(
-        jnp.broadcast_to(shard[None], (peers, *shard.shape)), axis, 0, 0, tiled=True
-    )
-
-
-def collect(shard, axis, dim):
-    return joined_along(copy_for_each(shard, axis), dim)
-
-
-def in_blocks(shard, dim, peers):
-    before, after = (shard.shape[:dim], shard.shape[dim + 1 :])
-    return jnp.moveaxis(shard.reshape(*before, peers, -1, *after), dim, 0)
-
-
-def summed_on_arrival(shard, axis, dim):
-    pieces = in_blocks(shard, dim, lax.axis_size(axis))
-    arrived = lax.all_to_all(pieces, axis, split_axis=0, concat_axis=0, tiled=True)
-    return arrived.astype(jnp.float32).sum(axis=0)
 
 
 def body(hidden, norm_gain, expert_ids, router_logits, w_gate, w_up, w_down):
@@ -56,19 +28,17 @@
     gate_mat = w_gate[0]
     up_mat = w_up[0]
     down_mat = w_down[0]
-    nearby = collect(arrived, "dp", 0)
-    block_rows = lax.all_gather(nearby, "tp", axis=0, tiled=True)
+    block_rows = lax.all_gather(arrived, ("tp", "dp"), axis=0, tiled=True)
     gate_val = jnp.dot(block_rows, gate_mat, preferred_element_type=jnp.float32)
     up_val = jnp.dot(block_rows, up_mat, preferred_element_type=jnp.float32)
     activations = (jax.nn.silu(gate_val) * up_val).astype(jnp.bfloat16)
     partial_sum = lax.psum_scatter(
         jnp.dot(activations, down_mat, preferred_element_type=jnp.float32).astype(jnp.bfloat16),
-        "tp",
+        ("tp", "dp"),
         scatter_dimension=0,
         tiled=True,
     )
-    summed = summed_on_arrival(partial_sum, "dp", 0)
-    outgoing = summed.astype(jnp.bfloat16).reshape(groups, MOST, width)
+    outgoing = partial_sum.reshape(groups, MOST, width)
     returned = lax.all_to_all(outgoing, "expert", split_axis=0, concat_axis=0, tiled=True)
     picked = jnp.dot(
         selector.T, returned.reshape(groups * MOST, width), preferred_element_type=jnp.float32

time: 185 us -> 212 us (1.15)
  waiting for transfers between devices: 93.1 us -> 153 us
  blocking collectives: 51.6 us -> 18.7 us
    reduce_scatter x1, waiting for transfers between devices: 45.3 us -> 93.6 us  [body(): lax.psum_scatter(jnp.dot(activations, down_mat, preferred_element_type=jn...]
    all_to_all x2 -> x0, blocking collectives: 32.8 us -> none  [the longest x1 17.9 us: summed_on_arrival(): lax.all_to_all(pieces, axis, split_axis=0, concat_axis=0, tiled=True)]
    all_gather x1, waiting for transfers between devices: 37.3 us -> 49.3 us  [body(): block_rows = lax.all_gather(arrived, ('tp', 'dp'), axis=0, tiled=True)]
where the time goes in v1:
time: 212 us
  waiting for transfers between devices  153 us (72%)
  blocking collectives  18.7 us (9%)
  between operations  13.5 us (6%)
  matrix products  12.9 us (6%)
  starting transfers between devices  7.06 us (3%)
  local copies, waits for them, and re-layouts  4.7 us (2%)
  other arithmetic  2.2 us (1%)
    reduce_scatter x1, waiting for transfers between devices, body(): lax.psum_scatter(jnp.dot(activations, down_mat, preferred_element_type=jn...  93.6 us
    all_gather x1, waiting for transfers between devices, body(): block_rows = lax.all_gather(arrived, ('tp', 'dp'), axis=0, tiled=True)  49.3 us
    all_to_all x1, blocking collectives, body(): lax.all_to_all(bucket.reshape(groups, MOST, width), 'expert', split_axis=...  18.7 us
    all_to_all x1, waiting for transfers between devices, body(): lax.all_to_all(outgoing, 'expert', split_axis=0, concat_axis=0, tiled=True)  9.65 us
    all_to_all x1, starting transfers between devices, body(): lax.all_to_all(outgoing, 'expert', split_axis=0, concat_axis=0, tiled=True)  7.02 us
    dot_general x1, matrix products, body(): gate_val = jnp.dot(block_rows, gate_mat, preferred_element_type=jnp.float32)  5.64 us
    dot_general x1, matrix products, body(): jnp.dot(activations, down_mat, preferred_element_type=jnp.float32)  4.48 us
  transfers between devices with their start and end apart: 3, of which 3 were waited for; matrix products, arithmetic and copies ran while one was open for 0% of the time, Pallas kernels for 0%

profile of v1, /device:TPU:6, one launch (start us, length us, event | category | flops | bytes accessed | tf_op | source)
XLA Modules:
  0.0 211.7 jit_solution(10548735742727239123)
XLA Ops:
  6.5 0.9 copy.14
  7.5 0.1 eq.51
  7.5 0.1 iota_compare_fusion.1
  7.6 0.2 select_reduce_fusion
  7.9 1.0 fusion.12
  8.8 0.9 fusion.14
  9.7 0.1 broadcast_in_dim.2
  9.9 0.2 convolution_convert_fusion.1
  10.0 0.1 reshape.92
  10.2 18.7 %all_to_all.10 = bf16[8,2,6144]{2,1,0:T(2,128)(2,1)S(1)} all-to-all(bf16[8,2,6144]{2,1,0:T(2,128)(2,1)S(1)} %reshape.92), channel_id=1, replica_groups=mesh['expert'=8,'tp'=8,'dp'=4] {'expert'}, dimensions={0} | all-to-all | bytes 393216 | tf_op jit(solution)/shard_map/all_to_all | solution.py:24
  28.9 0.7 reshape.93
  29.7 0.0 reduce-scatter.2.cloned.1.call-start
  29.8 49.3 %all-gather.2.cloned.1.call-done = bf16[512,6144]{1,0:T(8,128)(2,1)} async-done(((bf16[16,6144]{1,0:T(8,128)(2,1)}), bf16[512,6144]{1,0:T(8,128)(2,1)}) %all-gather.2.cloned.1.call-update) | async-done | bytes 6291472 | tf_op jit(solution)/shard_map/all_gather | solution.py:31
  79.1 5.6 %fusion.3 = f32[512,256]{1,0:T(8,128)S(1)} fusion(bf16[512,6144]{1,0:T(8,128)(2,1)} %all-gather.2.cloned.1.call-done, bf16[1,6144,256]{2,1,0:T(8,128)(2,1)} %param.11), kind=kOutput, calls=%fused_computation.6 | convolution fusion | flops 1610612736 | bytes 9961472 | tf_op jit(solution)/shard_map/dot_general | solution.py:32
  84.8 0.8 copy-done.3
  85.5 1.8 fusion.8
  87.3 4.5 %convolution_convert_fusion = bf16[512,6144]{1,0:T(8,128)(2,1)} fusion(bf16[512,256]{1,0:T(8,128)(2,1)S(1)} %fusion.8, bf16[1,256,6144]{2,1,0:T(8,128)(2,1)S(1)} %copy-done), kind=kOutput, calls=%fused_computation | convolution fusion | flops 1613758464 | bytes 9699328 | tf_op jit(solution)/shard_map/dot_general | solution.py:36
  91.8 93.6 %reduce-scatter.2.cloned.1.call-done = bf16[16,6144]{1,0:T(8,128)(2,1)} async-done(((bf16[512,6144]{1,0:T(8,128)(2,1)}), bf16[16,6144]{1,0:T(8,128)(2,1)}) %reduce-scatter.2.cloned.1.call-update) | async-done | bytes 196624 | tf_op jit(solution)/shard_map/reduce_scatter | solution.py:35
  185.4 1.7 reshape.94
  187.2 7.0 %all-to-all-start.1 = ((bf16[8,2,6144]{2,1,0:T(2,128)(2,1)}), bf16[8,2,6144]{2,1,0:T(2,128)(2,1)S(1)}, u32[]{:S(2)}, u32[]{:S(2)}) async-start(bf16[8,2,6144]{2,1,0:T(2,128)(2,1)} %reshape.94), calls=%async_computation.2 | async-start | bytes 393216 | tf_op jit(solution)/shard_map/all_to_all | solution.py:42
  194.2 0.1 copy.15
  194.3 9.6 %all-to-all-done.1 = bf16[8,2,6144]{2,1,0:T(2,128)(2,1)S(1)} async-done(((bf16[8,2,6144]{2,1,0:T(2,128)(2,1)}), bf16[8,2,6144]{2,1,0:T(2,128)(2,1)S(1)}, u32[]{:S(2)}, u32[]{:S(2)}) %all-to-all-start.1) | async-done | bytes 196640 | tf_op jit(solution)/shard_map/all_to_all | solution.py:42
  204.0 0.1 reshape.96
  204.0 0.8 fusion.11
  (19 shorter events, 0.2 us)
Async XLA Ops:
  6.5 80.8 %copy-start = (bf16[1,256,6144]{2,1,0:T(8,128)(2,1)S(1)}, bf16[1,256,6144]{2,1,0:T(8,128)(2,1)}, u32[]{:S(2)}) copy-start(bf16[1,256,6144]{2,1,0:T(8,128)(2,1)} %param.13) | copy-start | bytes 9437188
  6.5 72.6 %all-gather.2.cloned.1.call-start = ((), (), s32[]{:S(2)}) async-start(), calls=%async_computation.3 | async-start | bytes 6488064 | tf_op jit(solution)/shard_map/all_gather | solution.py:31
  29.7 155.7 %reduce-scatter.2.cloned.1.call-start = ((), (), s32[]{:S(2)}) async-start(), calls=%async_computation.4 | async-start | bytes 6488064 | tf_op jit(solution)/shard_map/reduce_scatter | solution.py:35
  79.1 5.7 %copy-start.2 = (bf16[512,6144]{1,0:T(8,128)(2,1)S(1)}, bf16[512,6144]{1,0:T(8,128)(2,1)}, u32[]{:S(2)}) copy-start(bf16[512,6144]{1,0:T(8,128)(2,1)} %all-gather.2.cloned.1.call-done) | copy-start | bytes 18874372
  79.1 6.4 %copy-start.3 = (bf16[1,6144,256]{2,1,0:T(8,128)(2,1)S(1)}, bf16[1,6144,256]{2,1,0:T(8,128)(2,1)}, u32[]{:S(2)}) copy-start(bf16[1,6144,256]{2,1,0:T(8,128)(2,1)} %param.12) | copy-start | bytes 9437188
  91.8 102.5 %copy-start.1 = (f32[4,2]{0,1:T(2,128)S(1)}, f32[4,2]{0,1:T(2,128)}, u32[]{:S(2)}) copy-start(f32[4,2]{0,1:T(2,128)} %param.10) | copy-start | bytes 100
  187.2 16.8 %all-to-all-start.1 = ((bf16[8,2,6144]{2,1,0:T(2,128)(2,1)}), bf16[8,2,6144]{2,1,0:T(2,128)(2,1)S(1)}, u32[]{:S(2)}, u32[]{:S(2)}) async-start(bf16[8,2,6144]{2,1,0:T(2,128)(2,1)} %reshape.94), calls=%async_computation.2 | async-start | bytes 393216 | tf_op jit(solution)/shard_map/all_to_all | solution.py:42
Sparse Core Ops, SparseCore 0:
  29.8 49.2 all-gather.1
  91.9 93.4 reduce-scatter.1
